TPU v7x, 256 devices: a whole 4x4x8 slice. The times are simulated.
256 devices in a mesh: ctx: 8 (over y, core), exp: 32 (over z, x).
Axes of the slice: x: 4, y: 4, z: 8, core: 2. Of those that a mesh axis runs over, the one named last changes fastest.
Arguments:
- hits: bfloat16 [32768, 2048], P(('ctx', 'exp')), may hold values from -6 to 6
- cotangent: bfloat16 [32768, 2048], P(('ctx', 'exp')), may hold values from -6 to 6
- combine: float32 [32768, 2], P(('ctx', 'exp')), may hold values from 0.1 to 1
- expert_ids: int32 [32768, 2], P(('ctx', 'exp')), may hold values from 0 to 31, all different within a row; in each aligned block of 128 rows (0 to 127, 128 to 255, ...) at most 12 rows name the same one
- gate_weight: bfloat16 [32, 2048, 768], P('exp'), may hold values from -0.125 to 0.125
- up_weight: bfloat16 [32, 2048, 768], P('exp'), may hold values from -0.125 to 0.125
- down_weight: bfloat16 [32, 2048, 768], P('exp'), may hold values from -0.21875 to 0.21875
Outputs:
- mixed: bfloat16 [32768, 2048], P(('ctx', 'exp'))
- input_grads: bfloat16 [32768, 2048], P(('ctx', 'exp'))
- combine_grads: float32 [32768, 2], P(('ctx', 'exp'))
- gate_grads: bfloat16 [32, 2048, 768], P('exp', 'ctx')
- up_grads: bfloat16 [32, 2048, 768], P('exp', 'ctx')
- down_grads: bfloat16 [32, 2048, 768], P('exp', 'ctx')
Inputs may be any that keep to these rules, and one draw needn't show every extreme that they name: `expert_ids`: the two ids of a hit differ. Among the 128 hits of one device no expert is named more than 12 times, and in every draw some device names some expert exactly 12 times.
All inputs are finite; a program needn't handle non-finite values.
Results may differ from a plain program's by a relative error of at most 0.017.
Values may be sent and summed in bfloat16 or wider, within the bound.
A program may use at most 128 MiB of HBM per device.

v0:
```python
import functools

import jax
import jax.numpy as jnp
from jax import lax
from jax.experimental import pallas as pl
from jax.experimental.pallas import tpu as pltpu
from jax.sharding import PartitionSpec as P

MESH = pl.DeviceIdType.MESH
F32 = jnp.float32
BF16 = jnp.bfloat16

grad_scale = 0.0625
NZ, NX, NY = 8, 4, 4
EXPERTS = NZ * NX
CAP = 12
T = 128
D = 2048
FF = 768
RB = 16
Q = 512
W = 3 * Q
ROWS = EXPERTS * RB
CS = D // 8
HALF = CS // 2
DYS = (2, 1, 3, 0)


def shift_order():
    order = []
    for dx in range(NX):
        for dz in (1, 7, 2, 6, 3, 5, 4, 0):
            if (dz, dx) != (0, 0):
                order.append((dz, dx))
    return order


def nn(a, b):
    return jnp.dot(a, b, preferred_element_type=F32)


def nt(a, b):
    return lax.dot_general(a, b, (((1,), (1,)), ((), ())), preferred_element_type=F32)


def tn(a, b):
    return lax.dot_general(a, b, (((0,), (0,)), ((), ())), preferred_element_type=F32)


def iota(shape, dim):
    return lax.broadcasted_iota(jnp.int32, shape, dim)


def bits(cond):
    return jnp.where(cond, 1.0, 0.0).astype(BF16)


def kernel(
    hits, cotangent, combine, expert_ids, wg_hbm, wu_hbm, wd_hbm,
    mixed_out, igrad_out, cgrad_out, gate_out, up_out, down_out,
    wg, wu, wd, send, recv, xs, cs, act, fac, hid, gg, gu,
    po, pr, st, ra, rb, r1, r3,
    w_sem, send_sem, recv_sem, po_sem, pr_sem, y_send, y_recv,
):
    c = lax.axis_index("ctx")
    me = lax.axis_index("exp")
    z, x = me // NX, me % NX
    y, core = c // 2, c % 2
    sibling = y * 2 + 1 - core
    y_next = ((y + 1) % NY) * 2 + core
    y_prev = ((y + NY - 1) % NY) * 2 + core
    order = shift_order()

    def peer(dz, dx):
        return ((z + dz) % NZ) * NX + (x + dx) % NX

    loads = []
    for i, (src, dst) in enumerate(((wg_hbm, wg), (wu_hbm, wu), (wd_hbm, wd))):
        copy = pltpu.make_async_copy(src.at[0], dst, w_sem.at[i])
        copy.start()
        loads.append(copy)

    barrier = pltpu.get_barrier_semaphore()
    for dz, dx in order:
        pl.semaphore_signal(barrier, inc=1, device_id=(c, peer(dz, dx)), device_id_type=MESH)
    for other in (sibling, y_next, y_prev):
        pl.semaphore_signal(barrier, inc=1, device_id=(other, me), device_id_type=MESH)

    lane = iota((T, 128), 1)
    ids = [expert_ids[:, k : k + 1] for k in range(2)]
    named = bits((lane == ids[0]) | (lane == ids[1]))
    earlier = bits(iota((T, T), 1) < iota((T, T), 0))
    before = nn(earlier, named)
    s_col, v_col = [], []
    for k in range(2):
        rank = jnp.sum(jnp.where(lane == ids[k], before, 0.0), axis=1, keepdims=True).astype(jnp.int32)
        block = (((ids[k] >> 2) - z) & (NZ - 1)) * NX + (((ids[k] & (NX - 1)) - x) & (NX - 1))
        s_col.append(block * RB + rank)
        v_col.append((rank >> 2) * ROWS + block * RB + CAP + (rank & 3))
    table = jnp.where(lane == 0, s_col[0], jnp.where(lane == 1, s_col[1], jnp.where(lane == 2, v_col[0], v_col[1])))
    turned = jnp.transpose(table.astype(F32)).astype(jnp.int32)
    s_row = [turned[k : k + 1, :] for k in range(2)]
    v_row = [turned[2 + k : 3 + k, :] for k in range(2)]
    rows_t = iota((ROWS, T), 0)

    def copies(phase, back, src, dst):
        for dz, dx in order:
            i = dz * NX + dx
            to = peer(NZ - dz, NX - dx) if back else peer(dz, dx)
            pltpu.make_async_remote_copy(
                src_ref=src.at[pl.ds(RB * i, RB)],
                dst_ref=dst.at[pl.ds(RB * i, RB)],
                send_sem=send_sem.at[phase],
                recv_sem=recv_sem.at[phase],
                device_id=(c, to),
                device_id_type=MESH,
            ).start()
        dst[0:RB, :] = src[0:RB, :]

    def whole(phase):
        return pltpu.make_async_remote_copy(
            src_ref=send.at[phase, pl.ds(RB, ROWS - RB)],
            dst_ref=recv.at[phase, pl.ds(RB, ROWS - RB)],
            send_sem=send_sem.at[phase],
            recv_sem=recv_sem.at[phase],
            device_id=(c, peer(1, 0)),
            device_id_type=MESH,
        )

    d_any = bits((rows_t == s_row[0]) | (rows_t == s_row[1]))
    for b in range(3):
        t_any = bits((rows_t + ROWS * b == v_row[0]) | (rows_t + ROWS * b == v_row[1]))
        left = jnp.concatenate([d_any, t_any], axis=1)
        right = jnp.concatenate([hits[:, Q * b : Q * b + Q], hits[:, W:]], axis=0)
        send[0, :, Q * b : Q * b + Q] = nn(left, right).astype(BF16)
    pl.semaphore_wait(barrier, len(order) + 3)
    copies(0, False, send.at[0], recv.at[0])

    for b in range(3):
        left, right = [], []
        for k in range(2):
            weight = combine[:, k : k + 1]
            left.append(bits(rows_t == s_row[k]))
            right.append((weight * cotangent[:, Q * b : Q * b + Q].astype(F32)).astype(BF16))
            left.append(bits(rows_t + ROWS * b == v_row[k]))
            right.append((weight * cotangent[:, W:].astype(F32)).astype(BF16))
        send[1, :, Q * b : Q * b + Q] = nn(
            jnp.concatenate(left, axis=1), jnp.concatenate(right, axis=0)
        ).astype(BF16)
    whole(0).wait_send()
    copies(1, False, send.at[1], recv.at[1])

    row = iota((256, 256), 0)
    col = iota((256, 256), 1)
    same = (row >> 4) == (col >> 4)
    keep = jnp.where((iota((256, 1), 0) & 15) < CAP, 1.0, 0.0)
    keep_all = jnp.where((iota((ROWS, 1), 0) & 15) < CAP, 1.0, 0.0)

    def unpack(src, dst):
        for h in range(ROWS // 256):
            part = pl.ds(256 * h, 256)
            tail = jnp.zeros((256, Q), F32)
            for b in range(3):
                block = src[part, Q * b : Q * b + Q]
                dst[part, Q * b : Q * b + Q] = (block.astype(F32) * keep).astype(BF16)
                pick = bits(
                    same & ((row & 15) < CAP) & (((row & 15) >> 2) == b) & ((col & 15) == CAP + (row & 3))
                )
                tail = tail + nn(pick, block)
            dst[part, W:] = tail.astype(BF16)

    def pack(product, dst):
        tail = product(3).astype(BF16)
        for b in range(3):
            main = product(b) * keep_all
            pick = bits(same & ((row & 15) >= CAP) & ((col & 15) == 4 * b + (row & 15) - CAP))
            for h in range(ROWS // 256):
                dst[256 * h : 256 * h + 256, Q * b : Q * b + Q] = (
                    main[256 * h : 256 * h + 256] + nn(pick, tail[256 * h : 256 * h + 256])
                ).astype(BF16)

    whole(0).wait_recv()
    unpack(recv.at[0], xs)
    loads[0].wait()
    loads[1].wait()

    @pl.loop(0, FF // 256)
    def _(n):
        part = pl.ds(pl.multiple_of(n * 256, 256), 256)
        gate = nn(xs[...], wg[:, part])
        up = nn(xs[...], wu[:, part])
        sig = jax.nn.sigmoid(gate)
        active = gate * sig
        act[:, part] = active
        fac[:, part] = up * sig * (1.0 + gate * (1.0 - sig))
        hid[:, part] = (active * up).astype(BF16)

    loads[2].wait()
    pack(lambda b: nt(hid[...], wd[Q * b : Q * b + Q, :]), send.at[2])
    whole(1).wait_send()
    copies(2, True, send.at[2], recv.at[2])

    whole(1).wait_recv()
    unpack(recv.at[1], cs)

    @pl.loop(0, FF // 256)
    def _(n):
        part = pl.ds(pl.multiple_of(n * 256, 256), 256)
        grad_hidden = nn(cs[...], wd[:, part])
        gu[:, part] = (grad_hidden * act[:, part]).astype(BF16)
        gg[:, part] = (grad_hidden * fac[:, part]).astype(BF16)

    def weight_terms(owner):
        part = pl.ds(pl.multiple_of(owner * CS, CS), CS)
        return (
            tn(xs[:, part], gg[...]),
            tn(xs[:, part], gu[...]),
            tn(cs[:, part], hid[...]),
        )

    over = []
    for j, dy in enumerate(DYS):
        terms = weight_terms(((y + dy) % NY) * 2 + 1 - core)
        for i in range(3):
            po[j, :, FF * i : FF * i + FF] = terms[i].astype(BF16)
        copy = pltpu.make_async_remote_copy(
            src_ref=po.at[j],
            dst_ref=pr.at[j],
            send_sem=po_sem.at[j],
            recv_sem=pr_sem.at[j],
            device_id=(sibling, me),
            device_id_type=MESH,
        )
        copy.start()
        over.append(copy)

    pack(
        lambda b: nt(gg[...], wg[Q * b : Q * b + Q, :]) + nt(gu[...], wu[Q * b : Q * b + Q, :]),
        send.at[3],
    )
    copies(3, True, send.at[3], recv.at[3])

    def along(i, src, dst, to):
        return pltpu.make_async_remote_copy(
            src_ref=src,
            dst_ref=dst,
            send_sem=y_send.at[i],
            recv_sem=y_recv.at[i],
            device_id=(to, me),
            device_id_type=MESH,
        )

    top, low = pl.ds(0, HALF), pl.ds(HALF, HALF)
    hops = [
        along(0, st.at[0, top], ra, y_next),
        along(1, st.at[0, low], rb, y_prev),
        along(2, st.at[1, low], r1.at[low], y_next),
        along(3, st.at[2, top], r3.at[top], y_prev),
        along(4, st.at[1, top], r1.at[top], y_next),
        along(5, st.at[2, low], r3.at[low], y_prev),
    ]
    for j, dy in enumerate(DYS[:3]):
        terms = weight_terms(((y + dy) % NY) * 2 + core)
        over[j].wait_recv()
        for i in range(3):
            part = slice(FF * i, FF * i + FF)
            st[j, :, part] = (terms[i] + pr[j, :, part].astype(F32)).astype(BF16)
        if j == 0:
            hops[0].start()
            hops[1].start()
        else:
            hops[1 + j].start()
    hops[0].wait_recv()
    st[1, top, :] = (st[1, top, :].astype(F32) + ra[...].astype(F32)).astype(BF16)
    hops[4].start()
    hops[1].wait_recv()
    st[2, low, :] = (st[2, low, :].astype(F32) + rb[...].astype(F32)).astype(BF16)
    hops[5].start()

    lane_s = iota((T, ROWS), 1)
    s_pick = [bits(lane_s == s_col[k]) for k in range(2)]
    v_pick = [[bits(lane_s + ROWS * b == v_col[k]) for b in range(3)] for k in range(2)]
    whole(2).wait_recv()
    sums = [jnp.zeros((T, 1), F32) for _ in range(2)]
    for b in range(4):
        total = jnp.zeros((T, Q), F32)
        cot = cotangent[:, Q * b : Q * b + Q].astype(F32)
        for k in range(2):
            if b < 3:
                rows = nn(s_pick[k], recv[2, :, Q * b : Q * b + Q])
            else:
                rows = nn(v_pick[k][0], recv[2, :, 0:Q])
                rows = rows + nn(v_pick[k][1], recv[2, :, Q : 2 * Q])
                rows = rows + nn(v_pick[k][2], recv[2, :, 2 * Q : W])
            total = total + combine[:, k : k + 1] * rows
            sums[k] = sums[k] + jnp.sum(cot * rows, axis=1, keepdims=True)
        mixed_out[:, Q * b : Q * b + Q] = total.astype(BF16)
    cgrad_out[...] = jnp.where(iota((T, 2), 1) == 0, sums[0], sums[1])

    terms = weight_terms(c)
    over[3].wait_recv()
    for i in (2, 3, 4, 5):
        hops[i].wait_recv()
    for i, out in enumerate((gate_out, up_out, down_out)):
        part = slice(FF * i, FF * i + FF)
        total = terms[i] + pr[3, :, part].astype(F32) + r1[:, part].astype(F32) + r3[:, part].astype(F32)
        out[0] = (total * grad_scale).astype(BF16)

    s_both = bits((lane_s == s_col[0]) | (lane_s == s_col[1]))
    whole(3).wait_recv()
    for b in range(3):
        igrad_out[:, Q * b : Q * b + Q] = nn(s_both, recv[3, :, Q * b : Q * b + Q]).astype(BF16)
    tail = jnp.zeros((T, Q), F32)
    for b in range(3):
        v_both = bits((lane_s + ROWS * b == v_col[0]) | (lane_s + ROWS * b == v_col[1]))
        tail = tail + nn(v_both, recv[3, :, Q * b : Q * b + Q])
    igrad_out[:, W:] = tail.astype(BF16)

    whole(2).wait_send()
    whole(3).wait_send()
    for copy in over:
        copy.wait_send()
    for copy in hops:
        copy.wait_send()


def local(hits, cotangent, combine, expert_ids, gate_weight, up_weight, down_weight):
    vmem = pl.BlockSpec(memory_space=pltpu.VMEM)
    hbm = pl.BlockSpec(memory_space=pl.ANY)
    shape = jax.ShapeDtypeStruct
    return pl.pallas_call(
        kernel,
        out_shape=(
            shape((T, D), BF16),
            shape((T, D), BF16),
            shape((T, 2), F32),
            shape((1, CS, FF), BF16),
            shape((1, CS, FF), BF16),
            shape((1, CS, FF), BF16),
        ),
        in_specs=[vmem, vmem, vmem, vmem, hbm, hbm, hbm],
        out_specs=(vmem,) * 6,
        scratch_shapes=[
            pltpu.VMEM((D, FF), BF16),
            pltpu.VMEM((D, FF), BF16),
            pltpu.VMEM((D, FF), BF16),
            pltpu.VMEM((4, ROWS, W), BF16),
            pltpu.VMEM((4, ROWS, W), BF16),
            pltpu.VMEM((ROWS, D), BF16),
            pltpu.VMEM((ROWS, D), BF16),
            pltpu.VMEM((ROWS, FF), F32),
            pltpu.VMEM((ROWS, FF), F32),
            pltpu.VMEM((ROWS, FF), BF16),
            pltpu.VMEM((ROWS, FF), BF16),
            pltpu.VMEM((ROWS, FF), BF16),
            pltpu.VMEM((4, CS, 3 * FF), BF16),
            pltpu.VMEM((4, CS, 3 * FF), BF16),
            pltpu.VMEM((3, CS, 3 * FF), BF16),
            pltpu.VMEM((HALF, 3 * FF), BF16),
            pltpu.VMEM((HALF, 3 * FF), BF16),
            pltpu.VMEM((CS, 3 * FF), BF16),
            pltpu.VMEM((CS, 3 * FF), BF16),
            pltpu.SemaphoreType.DMA((3,)),
            pltpu.SemaphoreType.DMA((4,)),
            pltpu.SemaphoreType.DMA((4,)),
            pltpu.SemaphoreType.DMA((4,)),
            pltpu.SemaphoreType.DMA((4,)),
            pltpu.SemaphoreType.DMA((6,)),
            pltpu.SemaphoreType.DMA((6,)),
        ],
        compiler_params=pltpu.CompilerParams(
            collective_id=0, has_side_effects=True, vmem_limit_bytes=64 << 20
        ),
        name="expert_step",
    )(hits, cotangent, combine, expert_ids, gate_weight, up_weight, down_weight)


def solution(mesh):
    rows = P(("ctx", "exp"), None)
    placed = (rows, rows, rows, rows, P("exp", None, None), P("exp", None, None), P("exp", None, None))
    outs = (rows, rows, rows, P("exp", "ctx", None), P("exp", "ctx", None), P("exp", "ctx", None))
    return jax.shard_map(local, mesh=mesh, in_specs=placed, out_specs=outs, check_vma=False)
```

profile of v0, /device:TPU:32, one launch (start us, length us, event | category | flops | bytes accessed | tf_op | source)
XLA Modules:
  0.0 162.1 jit_solution(10492456599914747259)
XLA Ops:
  0.6 1.4 copy.13.combine
  2.0 1.4 copy.14.expert_ids
  3.5 150.0 %expert_step.1 = (bf16[128,2048]{1,0:T(8,128)(2,1)}, bf16[128,2048]{1,0:T(8,128)(2,1)}, f32[128,2]{1,0:T(8,128)}, bf16[1,256,768]{2,1,0:T(8,128)(2,1)}, bf16[1,2...) custom-call(bf16[128,2048]{1,0:T(8,128)(2,1)} %hits.1, bf16[128,2048]{1,0:T(8,128)(2,1)} %cotangent.1, ...), custom_call_target="tpu_custom_call" | custom-call | tf_op jit(solution)/shard_map/expert_step/pallas_call | solution.py:332
  153.5 0.0 copy-start.1
  153.5 0.0 copy-start
  153.5 1.5 copy.15
  155.0 1.9 %copy.21 = bf16[128,2048]{1,0:T(8,128)(2,1)} copy(bf16[128,2048]{1,0:T(8,128)(2,1)} %get-tuple-element.18) | data formatting | bytes 1048576
  156.9 1.9 %copy.22 = bf16[128,2048]{1,0:T(8,128)(2,1)} copy(bf16[128,2048]{1,0:T(8,128)(2,1)} %get-tuple-element.19) | data formatting | bytes 1048576
  158.8 1.8 %copy.23 = bf16[1,256,768]{2,1,0:T(8,128)(2,1)} copy(bf16[1,256,768]{2,1,0:T(8,128)(2,1)} %get-tuple-element.21) | data formatting | bytes 786432
  160.6 0.0 copy-done.1
  160.6 0.7 copy.24
  161.3 0.0 copy-done
  161.3 0.7 copy.25
Async XLA Ops:
  153.5 7.1 %copy-start.1 = (bf16[1,256,768]{2,1,0:T(8,128)(2,1)S(1)}, bf16[1,256,768]{2,1,0:T(8,128)(2,1)}, u32[]{:S(2)}) copy-start(bf16[1,256,768]{2,1,0:T(8,128)(2,1)} %get-tuple-element.22) | copy-start | bytes 1179652
  153.5 7.8 %copy-start = (bf16[1,256,768]{2,1,0:T(8,128)(2,1)S(1)}, bf16[1,256,768]{2,1,0:T(8,128)(2,1)}, u32[]{:S(2)}) copy-start(bf16[1,256,768]{2,1,0:T(8,128)(2,1)} %get-tuple-element.23) | copy-start | bytes 1179652
where the time goes:
time: 162 us
  Pallas kernels  150 us (93%)
  local copies, waits for them, and re-layouts  11.4 us (7%)
    pallas_call x1, Pallas kernels, local(): pl.pallas_call(kernel, out_shape=(shape((T, D), BF16), shape((T, D), BF16...  150 us
    unnamed x11, local copies, waits for them, and re-layouts  9.85 us

commit v1 on v0

--- a/solution.py
+++ b/solution.py
@@ -61,7 +61,8 @@
     mixed_out, igrad_out, cgrad_out, gate_out, up_out, down_out,
     wg, wu, wd, send, recv, xs, cs, act, fac, hid, gg, gu,
     po, pr, st, ra, rb, r1, r3,
-    w_sem, send_sem, recv_sem, po_sem, pr_sem, y_send, y_recv,
+    mixed, igrad, cgrad, gate, up, down,
+    w_sem, send_sem, recv_sem, po_sem, pr_sem, y_send, y_recv, out_sem,
 ):
     c = lax.axis_index("ctx")
     me = lax.axis_index("exp")
@@ -87,21 +88,25 @@
     for other in (sibling, y_next, y_prev):
         pl.semaphore_signal(barrier, inc=1, device_id=(other, me), device_id_type=MESH)
 
-    lane = iota((T, 128), 1)
-    ids = [expert_ids[:, k : k + 1] for k in range(2)]
-    named = bits((lane == ids[0]) | (lane == ids[1]))
-    earlier = bits(iota((T, T), 1) < iota((T, T), 0))
-    before = nn(earlier, named)
-    s_col, v_col = [], []
+    name = iota((EXPERTS, T), 0)
+    ids = [expert_ids[k : k + 1, :] for k in range(2)]
+    named = bits((name == ids[0]) | (name == ids[1]))
+    earlier = bits(iota((T, T), 0) < iota((T, T), 1))
+    before = nn(named, earlier)
+    s_row, v_row = [], []
     for k in range(2):
-        rank = jnp.sum(jnp.where(lane == ids[k], before, 0.0), axis=1, keepdims=True).astype(jnp.int32)
+        rank = jnp.sum(jnp.where(name == ids[k], before, 0.0), axis=0, keepdims=True).astype(jnp.int32)
         block = (((ids[k] >> 2) - z) & (NZ - 1)) * NX + (((ids[k] & (NX - 1)) - x) & (NX - 1))
-        s_col.append(block * RB + rank)
-        v_col.append((rank >> 2) * ROWS + block * RB + CAP + (rank & 3))
-    table = jnp.where(lane == 0, s_col[0], jnp.where(lane == 1, s_col[1], jnp.where(lane == 2, v_col[0], v_col[1])))
-    turned = jnp.transpose(table.astype(F32)).astype(jnp.int32)
-    s_row = [turned[k : k + 1, :] for k in range(2)]
-    v_row = [turned[2 + k : 3 + k, :] for k in range(2)]
+        s_row.append(block * RB + rank)
+        v_row.append((rank >> 2) * ROWS + block * RB + CAP + (rank & 3))
+    meta = jnp.concatenate(
+        [r.astype(F32) for r in s_row + v_row] + [combine[0:1, :], combine[1:2, :], jnp.zeros((2, T), F32)],
+        axis=0,
+    )
+    turned = jnp.transpose(jnp.concatenate([meta] * (T // 8), axis=0))
+    s_col = [turned[:, k : k + 1].astype(jnp.int32) for k in range(2)]
+    v_col = [turned[:, 2 + k : 3 + k].astype(jnp.int32) for k in range(2)]
+    weights = [turned[:, 4 + k : 5 + k] for k in range(2)]
     rows_t = iota((ROWS, T), 0)
 
     def copies(phase, back, src, dst):
@@ -128,6 +133,13 @@
             device_id_type=MESH,
         )
 
+    left_over = []
+
+    def leave(i, src, dst):
+        copy = pltpu.make_async_copy(src, dst, out_sem.at[i])
+        copy.start()
+        left_over.append(copy)
+
     d_any = bits((rows_t == s_row[0]) | (rows_t == s_row[1]))
     for b in range(3):
         t_any = bits((rows_t + ROWS * b == v_row[0]) | (rows_t + ROWS * b == v_row[1]))
@@ -140,7 +152,7 @@
     for b in range(3):
         left, right = [], []
         for k in range(2):
-            weight = combine[:, k : k + 1]
+            weight = weights[k]
             left.append(bits(rows_t == s_row[k]))
             right.append((weight * cotangent[:, Q * b : Q * b + Q].astype(F32)).astype(BF16))
             left.append(bits(rows_t + ROWS * b == v_row[k]))
@@ -188,13 +200,13 @@
     @pl.loop(0, FF // 256)
     def _(n):
         part = pl.ds(pl.multiple_of(n * 256, 256), 256)
-        gate = nn(xs[...], wg[:, part])
-        up = nn(xs[...], wu[:, part])
-        sig = jax.nn.sigmoid(gate)
-        active = gate * sig
+        gates = nn(xs[...], wg[:, part])
+        ups = nn(xs[...], wu[:, part])
+        sig = jax.nn.sigmoid(gates)
+        active = gates * sig
         act[:, part] = active
-        fac[:, part] = up * sig * (1.0 + gate * (1.0 - sig))
-        hid[:, part] = (active * up).astype(BF16)
+        fac[:, part] = ups * sig * (1.0 + gates * (1.0 - sig))
+        hid[:, part] = (active * ups).astype(BF16)
 
     loads[2].wait()
     pack(lambda b: nt(hid[...], wd[Q * b : Q * b + Q, :]), send.at[2])
@@ -293,29 +305,33 @@
                 rows = nn(v_pick[k][0], recv[2, :, 0:Q])
                 rows = rows + nn(v_pick[k][1], recv[2, :, Q : 2 * Q])
                 rows = rows + nn(v_pick[k][2], recv[2, :, 2 * Q : W])
-            total = total + combine[:, k : k + 1] * rows
+            total = total + weights[k] * rows
             sums[k] = sums[k] + jnp.sum(cot * rows, axis=1, keepdims=True)
-        mixed_out[:, Q * b : Q * b + Q] = total.astype(BF16)
-    cgrad_out[...] = jnp.where(iota((T, 2), 1) == 0, sums[0], sums[1])
+        mixed[:, Q * b : Q * b + Q] = total.astype(BF16)
+    leave(0, mixed, mixed_out)
+    cgrad[...] = jnp.transpose(jnp.where(iota((T, 128), 1) == 0, sums[0], sums[1]))[0:2, :]
+    leave(1, cgrad, cgrad_out)
 
     terms = weight_terms(c)
     over[3].wait_recv()
     for i in (2, 3, 4, 5):
         hops[i].wait_recv()
-    for i, out in enumerate((gate_out, up_out, down_out)):
+    for i, (out, dst) in enumerate(((gate, gate_out), (up, up_out), (down, down_out))):
         part = slice(FF * i, FF * i + FF)
         total = terms[i] + pr[3, :, part].astype(F32) + r1[:, part].astype(F32) + r3[:, part].astype(F32)
         out[0] = (total * grad_scale).astype(BF16)
+        leave(2 + i, out, dst)
 
     s_both = bits((lane_s == s_col[0]) | (lane_s == s_col[1]))
     whole(3).wait_recv()
     for b in range(3):
-        igrad_out[:, Q * b : Q * b + Q] = nn(s_both, recv[3, :, Q * b : Q * b + Q]).astype(BF16)
+        igrad[:, Q * b : Q * b + Q] = nn(s_both, recv[3, :, Q * b : Q * b + Q]).astype(BF16)
     tail = jnp.zeros((T, Q), F32)
     for b in range(3):
         v_both = bits((lane_s + ROWS * b == v_col[0]) | (lane_s + ROWS * b == v_col[1]))
         tail = tail + nn(v_both, recv[3, :, Q * b : Q * b + Q])
-    igrad_out[:, W:] = tail.astype(BF16)
+    igrad[:, W:] = tail.astype(BF16)
+    leave(5, igrad, igrad_out)
 
     whole(2).wait_send()
     whole(3).wait_send()
@@ -323,24 +339,41 @@
         copy.wait_send()
     for copy in hops:
         copy.wait_send()
+    for copy in left_over:
+        copy.wait()
+
+
+def results(*refs):
+    ins, outs, held, sem = refs[:6], refs[6:12], refs[12:18], refs[18]
+    inward = [pltpu.make_async_copy(ins[i], held[i], sem.at[0, i]) for i in range(6)]
+    outward = [pltpu.make_async_copy(held[i], outs[i], sem.at[1, i]) for i in range(6)]
+    for copy in inward:
+        copy.start()
+    for before, after in zip(inward, outward):
+        before.wait()
+        after.start()
+    for copy in outward:
+        copy.wait()
 
 
 def local(hits, cotangent, combine, expert_ids, gate_weight, up_weight, down_weight):
     vmem = pl.BlockSpec(memory_space=pltpu.VMEM)
     hbm = pl.BlockSpec(memory_space=pl.ANY)
     shape = jax.ShapeDtypeStruct
-    return pl.pallas_call(
+    kinds = (
+        ((T, D), BF16),
+        ((T, D), BF16),
+        ((2, T), F32),
+        ((1, CS, FF), BF16),
+        ((1, CS, FF), BF16),
+        ((1, CS, FF), BF16),
+    )
+    outs = tuple(shape(*kind) for kind in kinds)
+    parts = pl.pallas_call(
         kernel,
-        out_shape=(
-            shape((T, D), BF16),
-            shape((T, D), BF16),
-            shape((T, 2), F32),
-            shape((1, CS, FF), BF16),
-            shape((1, CS, FF), BF16),
-            shape((1, CS, FF), BF16),
-        ),
+        out_shape=outs,
         in_specs=[vmem, vmem, vmem, vmem, hbm, hbm, hbm],
-        out_specs=(vmem,) * 6,
+        out_specs=(hbm,) * 6,
         scratch_shapes=[
             pltpu.VMEM((D, FF), BF16),
             pltpu.VMEM((D, FF), BF16),
@@ -361,6 +394,7 @@
             pltpu.VMEM((HALF, 3 * FF), BF16),
             pltpu.VMEM((CS, 3 * FF), BF16),
             pltpu.VMEM((CS, 3 * FF), BF16),
+            *[pltpu.VMEM(*kind) for kind in kinds],
             pltpu.SemaphoreType.DMA((3,)),
             pltpu.SemaphoreType.DMA((4,)),
             pltpu.SemaphoreType.DMA((4,)),
@@ -368,12 +402,22 @@
             pltpu.SemaphoreType.DMA((4,)),
             pltpu.SemaphoreType.DMA((6,)),
             pltpu.SemaphoreType.DMA((6,)),
+            pltpu.SemaphoreType.DMA((6,)),
         ],
         compiler_params=pltpu.CompilerParams(
             collective_id=0, has_side_effects=True, vmem_limit_bytes=64 << 20
         ),
         name="expert_step",
-    )(hits, cotangent, combine, expert_ids, gate_weight, up_weight, down_weight)
+    )(hits, cotangent, combine.T, expert_ids.T, gate_weight, up_weight, down_weight)
+    mixed, igrad, cgrad, gate, up, down = pl.pallas_call(
+        results,
+        out_shape=outs,
+        in_specs=[hbm] * 6,
+        out_specs=(hbm,) * 6,
+        scratch_shapes=[*[pltpu.VMEM(*kind) for kind in kinds], pltpu.SemaphoreType.DMA((2, 6))],
+        name="results",
+    )(*parts)
+    return mixed, igrad, cgrad.T, gate, up, down
 
 
 def solution(mesh):

time: 162 us -> 153 us (0.944)
  local copies, waits for them, and re-layouts: 11.4 us -> 0 us
  Pallas kernels: 150 us -> 152 us
    unnamed x11 -> x0, local copies, waits for them, and re-layouts: 9.85 us -> none
    pallas_call x1 -> x2, Pallas kernels: 150 us -> 152 us  [the longest x1 150 us: local(): pl.pallas_call(kernel, out_shape=outs, in_specs=[vmem, vmem, vmem, vmem,...]
where the time goes in v1:
time: 153 us
  Pallas kernels  152 us (99%)
    pallas_call x1, Pallas kernels, local(): pl.pallas_call(kernel, out_shape=outs, in_specs=[vmem, vmem, vmem, vmem,...  150 us

profile of v1, /device:TPU:32, one launch (start us, length us, event | category | flops | bytes accessed | tf_op | source)
XLA Modules:
  0.0 153.0 jit_solution(12119917564934210925)
XLA Ops:
  0.6 149.7 %expert_step.1 = (bf16[128,2048]{1,0:T(8,128)(2,1)}, bf16[128,2048]{1,0:T(8,128)(2,1)}, f32[2,128]{1,0:T(2,128)}, bf16[1,256,768]{2,1,0:T(8,128)(2,1)}, bf16[1,2...) custom-call(bf16[128,2048]{1,0:T(8,128)(2,1)} %hits.1, bf16[128,2048]{1,0:T(8,128)(2,1)} %cotangent.1, ...), custom_call_target="tpu_custom_call" | custom-call | tf_op jit(solution)/shard_map/expert_step/pallas_call | solution.py:372
  150.3 2.5 %results.1 = (bf16[128,2048]{1,0:T(8,128)(2,1)}, bf16[128,2048]{1,0:T(8,128)(2,1)}, f32[2,128]{1,0:T(2,128)}, bf16[1,256,768]{2,1,0:T(8,128)(2,1)}, bf16[1,256,7...) custom-call(bf16[128,2048]{1,0:T(8,128)(2,1)} %get-tuple-element.18.refs_0_, bf16[128,2048]{1,0:T(8,128)(2,1)} %get-tuple-element.19.refs_1_, ...), custom_call_target="tpu_custom_call" | custom-call | tf_op jit(solution)/shard_map/results/pallas_call | solution.py:412

commit v2 on v1

--- a/solution.py
+++ b/solution.py
@@ -27,13 +27,27 @@
 DYS = (2, 1, 3, 0)
 
 
-def shift_order():
+GROUPS = ((0, 64), (64, 288), (288, 512))
+WINDOWS = ((0, 128), (32, 256), (256, 256))
+SAME = (0, 4, 28)
+
+
+def hops_of():
+    table = {}
+    for dz in range(NZ):
+        for dx in range(NX):
+            i = dz * NX + dx
+            if dz == 0:
+                table[i] = (0, dx)
+            elif i * RB < GROUPS[1][1]:
+                table[i] = (dz - 1, dx)
+            else:
+                table[i] = (dz - NZ + 1, dx)
     order = []
     for dx in range(NX):
-        for dz in (1, 7, 2, 6, 3, 5, 4, 0):
-            if (dz, dx) != (0, 0):
-                order.append((dz, dx))
-    return order
+        for dz in (4, 3, 5, 2, 6, 1, 7, 0):
+            order.append(dz * NX + dx)
+    return [(i,) + table[i] for i in order if i not in SAME]
 
 
 def nn(a, b):
@@ -62,7 +76,9 @@
     wg, wu, wd, send, recv, xs, cs, act, fac, hid, gg, gu,
     po, pr, st, ra, rb, r1, r3,
     mixed, igrad, cgrad, gate, up, down,
+    metas, raw, own, part_to, part_from, cg_to, cg_from,
     w_sem, send_sem, recv_sem, po_sem, pr_sem, y_send, y_recv, out_sem,
+    raw_send, raw_recv, meta_send, meta_recv, part_send, part_recv, cg_send, cg_recv,
 ):
     c = lax.axis_index("ctx")
     me = lax.axis_index("exp")
@@ -71,10 +87,15 @@
     sibling = y * 2 + 1 - core
     y_next = ((y + 1) % NY) * 2 + core
     y_prev = ((y + NY - 1) % NY) * 2 + core
-    order = shift_order()
+    order = hops_of()
 
     def peer(dz, dx):
-        return ((z + dz) % NZ) * NX + (x + dx) % NX
+        return ((z + dz + NZ) % NZ) * NX + (x + dx + NX) % NX
+
+    def remote(src, dst, ssem, rsem, ctx, exp):
+        return pltpu.make_async_remote_copy(
+            src_ref=src, dst_ref=dst, send_sem=ssem, recv_sem=rsem, device_id=(ctx, exp), device_id_type=MESH
+        )
 
     loads = []
     for i, (src, dst) in enumerate(((wg_hbm, wg), (wu_hbm, wu), (wd_hbm, wd))):
@@ -83,7 +104,8 @@
         loads.append(copy)
 
     barrier = pltpu.get_barrier_semaphore()
-    for dz, dx in order:
+    near = [(dz, dx) for dz in range(-3, 4) for dx in range(NX) if (dz, dx) != (0, 0)]
+    for dz, dx in near:
         pl.semaphore_signal(barrier, inc=1, device_id=(c, peer(dz, dx)), device_id_type=MESH)
     for other in (sibling, y_next, y_prev):
         pl.semaphore_signal(barrier, inc=1, device_id=(other, me), device_id_type=MESH)
@@ -93,45 +115,96 @@
     named = bits((name == ids[0]) | (name == ids[1]))
     earlier = bits(iota((T, T), 0) < iota((T, T), 1))
     before = nn(named, earlier)
-    s_row, v_row = [], []
+    slots, tails = [], []
     for k in range(2):
         rank = jnp.sum(jnp.where(name == ids[k], before, 0.0), axis=0, keepdims=True).astype(jnp.int32)
         block = (((ids[k] >> 2) - z) & (NZ - 1)) * NX + (((ids[k] & (NX - 1)) - x) & (NX - 1))
-        s_row.append(block * RB + rank)
-        v_row.append((rank >> 2) * ROWS + block * RB + CAP + (rank & 3))
-    meta = jnp.concatenate(
-        [r.astype(F32) for r in s_row + v_row] + [combine[0:1, :], combine[1:2, :], jnp.zeros((2, T), F32)],
+        slots.append(block * RB + rank)
+        tails.append((rank >> 2) * ROWS + block * RB + CAP + (rank & 3))
+    metas[0] = jnp.concatenate(
+        [r.astype(F32) for r in slots + tails] + [combine[0:1, :], combine[1:2, :], jnp.zeros((2, T), F32)],
         axis=0,
     )
-    turned = jnp.transpose(jnp.concatenate([meta] * (T // 8), axis=0))
-    s_col = [turned[:, k : k + 1].astype(jnp.int32) for k in range(2)]
-    v_col = [turned[:, 2 + k : 3 + k].astype(jnp.int32) for k in range(2)]
-    weights = [turned[:, 4 + k : 5 + k] for k in range(2)]
-    rows_t = iota((ROWS, T), 0)
-
-    def copies(phase, back, src, dst):
-        for dz, dx in order:
-            i = dz * NX + dx
-            to = peer(NZ - dz, NX - dx) if back else peer(dz, dx)
-            pltpu.make_async_remote_copy(
-                src_ref=src.at[pl.ds(RB * i, RB)],
-                dst_ref=dst.at[pl.ds(RB * i, RB)],
-                send_sem=send_sem.at[phase],
-                recv_sem=recv_sem.at[phase],
-                device_id=(c, to),
-                device_id_type=MESH,
-            ).start()
-        dst[0:RB, :] = src[0:RB, :]
+
+    sides = ((peer(1, 0), peer(-1, 0)), (peer(-1, 0), peer(1, 0)))
+    metas_sent = [
+        remote(metas.at[0], metas.at[1 + i], meta_send.at[i], meta_recv.at[i], c, sides[i][0]) for i in range(2)
+    ]
+    raw_sent = [
+        [remote(src, raw.at[p, i], raw_send.at[p, i], raw_recv.at[p, i], c, sides[i][0]) for i in range(2)]
+        for p, src in enumerate((hits, cotangent))
+    ]
+    parts_sent = [
+        [
+            remote(part_to.at[p, i], part_from.at[p, i], part_send.at[p, i], part_recv.at[p, i], c, sides[i][1])
+            for i in range(2)
+        ]
+        for p in range(2)
+    ]
+    cg_sent = [remote(cg_to.at[i], cg_from.at[i], cg_send.at[i], cg_recv.at[i], c, sides[i][1]) for i in range(2)]
+
+    def rows_of(g):
+        meta = metas[g]
+        return (
+            [meta[k : k + 1, :].astype(jnp.int32) for k in range(2)],
+            [meta[2 + k : 3 + k, :].astype(jnp.int32) for k in range(2)],
+        )
+
+    def columns_of(g):
+        turned = jnp.transpose(jnp.concatenate([metas[g]] * (T // 8), axis=0))
+        return (
+            [turned[:, k : k + 1].astype(jnp.int32) for k in range(2)],
+            [turned[:, 2 + k : 3 + k].astype(jnp.int32) for k in range(2)],
+            [turned[:, 4 + k : 5 + k] for k in range(2)],
+        )
+
+    def copies(phase, back, blocks):
+        for i, dz, dx in order:
+            if i in blocks:
+                to = peer(-dz, -dx) if back else peer(dz, dx)
+                part = pl.ds(RB * i, RB)
+                remote(
+                    send.at[phase, part], recv.at[phase, part], send_sem.at[phase], recv_sem.at[phase], c, to
+                ).start()
+        for i in SAME:
+            if i in blocks:
+                recv[phase, RB * i : RB * i + RB, :] = send[phase, RB * i : RB * i + RB, :]
 
     def whole(phase):
-        return pltpu.make_async_remote_copy(
-            src_ref=send.at[phase, pl.ds(RB, ROWS - RB)],
-            dst_ref=recv.at[phase, pl.ds(RB, ROWS - RB)],
-            send_sem=send_sem.at[phase],
-            recv_sem=recv_sem.at[phase],
-            device_id=(c, peer(1, 0)),
-            device_id_type=MESH,
+        part = pl.ds(0, RB * len(order))
+        return remote(
+            send.at[phase, part], recv.at[phase, part], send_sem.at[phase], recv_sem.at[phase], c, peer(1, 0)
         )
+
+    near_blocks = range(0, GROUPS[0][1] // RB)
+    far_blocks = range(GROUPS[1][0] // RB, EXPERTS)
+
+    def pack_hits(g, src):
+        lo, hi = GROUPS[g]
+        s_row, v_row = rows_of(g)
+        rows = iota((hi - lo, T), 0) + lo
+        d_any = bits((rows == s_row[0]) | (rows == s_row[1]))
+        for b in range(3):
+            t_any = bits((rows + ROWS * b == v_row[0]) | (rows + ROWS * b == v_row[1]))
+            left = jnp.concatenate([d_any, t_any], axis=1)
+            right = jnp.concatenate([src[:, Q * b : Q * b + Q], src[:, W:]], axis=0)
+            send[0, lo:hi, Q * b : Q * b + Q] = nn(left, right).astype(BF16)
+
+    def pack_cots(g, src):
+        lo, hi = GROUPS[g]
+        s_row, v_row = rows_of(g)
+        weights = columns_of(g)[2]
+        rows = iota((hi - lo, T), 0) + lo
+        for b in range(3):
+            left, right = [], []
+            for k in range(2):
+                left.append(bits(rows == s_row[k]))
+                right.append((weights[k] * src[:, Q * b : Q * b + Q].astype(F32)).astype(BF16))
+                left.append(bits(rows + ROWS * b == v_row[k]))
+                right.append((weights[k] * src[:, W:].astype(F32)).astype(BF16))
+            send[1, lo:hi, Q * b : Q * b + Q] = nn(
+                jnp.concatenate(left, axis=1), jnp.concatenate(right, axis=0)
+            ).astype(BF16)
 
     left_over = []
 
@@ -140,28 +213,28 @@
         copy.start()
         left_over.append(copy)
 
-    d_any = bits((rows_t == s_row[0]) | (rows_t == s_row[1]))
-    for b in range(3):
-        t_any = bits((rows_t + ROWS * b == v_row[0]) | (rows_t + ROWS * b == v_row[1]))
-        left = jnp.concatenate([d_any, t_any], axis=1)
-        right = jnp.concatenate([hits[:, Q * b : Q * b + Q], hits[:, W:]], axis=0)
-        send[0, :, Q * b : Q * b + Q] = nn(left, right).astype(BF16)
-    pl.semaphore_wait(barrier, len(order) + 3)
-    copies(0, False, send.at[0], recv.at[0])
-
-    for b in range(3):
-        left, right = [], []
-        for k in range(2):
-            weight = weights[k]
-            left.append(bits(rows_t == s_row[k]))
-            right.append((weight * cotangent[:, Q * b : Q * b + Q].astype(F32)).astype(BF16))
-            left.append(bits(rows_t + ROWS * b == v_row[k]))
-            right.append((weight * cotangent[:, W:].astype(F32)).astype(BF16))
-        send[1, :, Q * b : Q * b + Q] = nn(
-            jnp.concatenate(left, axis=1), jnp.concatenate(right, axis=0)
-        ).astype(BF16)
+    pl.semaphore_wait(barrier, len(near) + 3)
+    for i in range(2):
+        metas_sent[i].start()
+        raw_sent[0][i].start()
+    pack_hits(0, hits)
+    copies(0, False, near_blocks)
+    pack_cots(0, cotangent)
+
+    for i in range(2):
+        metas_sent[i].wait_recv()
+        raw_sent[0][i].wait_recv()
+        if i == 0:
+            raw_sent[1][0].start()
+            raw_sent[1][1].start()
+        pack_hits(1 + i, raw.at[0, i])
+    copies(0, False, far_blocks)
+
+    for i in range(2):
+        raw_sent[1][i].wait_recv()
+        pack_cots(1 + i, raw.at[1, i])
     whole(0).wait_send()
-    copies(1, False, send.at[1], recv.at[1])
+    copies(1, False, range(EXPERTS))
 
     row = iota((256, 256), 0)
     col = iota((256, 256), 1)
@@ -211,7 +284,7 @@
     loads[2].wait()
     pack(lambda b: nt(hid[...], wd[Q * b : Q * b + Q, :]), send.at[2])
     whole(1).wait_send()
-    copies(2, True, send.at[2], recv.at[2])
+    copies(2, True, range(EXPERTS))
 
     whole(1).wait_recv()
     unpack(recv.at[1], cs)
@@ -236,14 +309,7 @@
         terms = weight_terms(((y + dy) % NY) * 2 + 1 - core)
         for i in range(3):
             po[j, :, FF * i : FF * i + FF] = terms[i].astype(BF16)
-        copy = pltpu.make_async_remote_copy(
-            src_ref=po.at[j],
-            dst_ref=pr.at[j],
-            send_sem=po_sem.at[j],
-            recv_sem=pr_sem.at[j],
-            device_id=(sibling, me),
-            device_id_type=MESH,
-        )
+        copy = remote(po.at[j], pr.at[j], po_sem.at[j], pr_sem.at[j], sibling, me)
         copy.start()
         over.append(copy)
 
@@ -251,17 +317,9 @@
         lambda b: nt(gg[...], wg[Q * b : Q * b + Q, :]) + nt(gu[...], wu[Q * b : Q * b + Q, :]),
         send.at[3],
     )
-    copies(3, True, send.at[3], recv.at[3])
 
     def along(i, src, dst, to):
-        return pltpu.make_async_remote_copy(
-            src_ref=src,
-            dst_ref=dst,
-            send_sem=y_send.at[i],
-            recv_sem=y_recv.at[i],
-            device_id=(to, me),
-            device_id_type=MESH,
-        )
+        return remote(src, dst, y_send.at[i], y_recv.at[i], to, me)
 
     top, low = pl.ds(0, HALF), pl.ds(HALF, HALF)
     hops = [
@@ -281,8 +339,55 @@
         if j == 0:
             hops[0].start()
             hops[1].start()
+            whole(2).wait_send()
+            copies(3, True, range(EXPERTS))
         else:
             hops[1 + j].start()
+
+    def picks(g):
+        lo, hi = GROUPS[g]
+        start, length = WINDOWS[g]
+        s_col, v_col, weights = columns_of(g)
+        lanes = iota((T, length), 1) + start
+        s_pick, v_pick = [], []
+        for k in range(2):
+            inside = (s_col[k] >= lo) & (s_col[k] < hi)
+            s_in = jnp.where(inside, s_col[k], -1)
+            v_in = jnp.where(inside, v_col[k], -1)
+            s_pick.append(lanes == s_in)
+            v_pick.append([lanes + ROWS * b == v_in for b in range(3)])
+        return s_pick, v_pick, weights
+
+    whole(2).wait_recv()
+    for g in (1, 2, 0):
+        s_pick, v_pick, weights = picks(g)
+        window = pl.ds(*WINDOWS[g])
+        source = cotangent if g == 0 else raw.at[1, g - 1]
+        sums = [jnp.zeros((T, 1), F32) for _ in range(2)]
+        for b in range(4):
+            total = jnp.zeros((T, Q), F32)
+            cot = source[:, Q * b : Q * b + Q].astype(F32)
+            for k in range(2):
+                if b < 3:
+                    rows = nn(bits(s_pick[k]), recv[2, window, Q * b : Q * b + Q])
+                else:
+                    rows = nn(bits(v_pick[k][0]), recv[2, window, 0:Q])
+                    rows = rows + nn(bits(v_pick[k][1]), recv[2, window, Q : 2 * Q])
+                    rows = rows + nn(bits(v_pick[k][2]), recv[2, window, 2 * Q : W])
+                total = total + weights[k] * rows
+                sums[k] = sums[k] + jnp.sum(cot * rows, axis=1, keepdims=True)
+            if g == 0:
+                own[0, :, Q * b : Q * b + Q] = total
+            else:
+                part_to[0, g - 1, :, Q * b : Q * b + Q] = total.astype(BF16)
+        pair = jnp.transpose(jnp.where(iota((T, 128), 1) == 0, sums[0], sums[1]))[0:8, :]
+        if g == 0:
+            own_pair = pair
+        else:
+            cg_to[g - 1] = pair
+            parts_sent[0][g - 1].start()
+            cg_sent[g - 1].start()
+
     hops[0].wait_recv()
     st[1, top, :] = (st[1, top, :].astype(F32) + ra[...].astype(F32)).astype(BF16)
     hops[4].start()
@@ -290,26 +395,32 @@
     st[2, low, :] = (st[2, low, :].astype(F32) + rb[...].astype(F32)).astype(BF16)
     hops[5].start()
 
-    lane_s = iota((T, ROWS), 1)
-    s_pick = [bits(lane_s == s_col[k]) for k in range(2)]
-    v_pick = [[bits(lane_s + ROWS * b == v_col[k]) for b in range(3)] for k in range(2)]
-    whole(2).wait_recv()
-    sums = [jnp.zeros((T, 1), F32) for _ in range(2)]
-    for b in range(4):
-        total = jnp.zeros((T, Q), F32)
-        cot = cotangent[:, Q * b : Q * b + Q].astype(F32)
-        for k in range(2):
+    whole(3).wait_recv()
+    for g in (1, 2, 0):
+        s_pick, v_pick, _ = picks(g)
+        window = pl.ds(*WINDOWS[g])
+        s_both = bits(s_pick[0] | s_pick[1])
+        v_both = [bits(v_pick[0][b] | v_pick[1][b]) for b in range(3)]
+        for b in range(4):
             if b < 3:
-                rows = nn(s_pick[k], recv[2, :, Q * b : Q * b + Q])
+                total = nn(s_both, recv[3, window, Q * b : Q * b + Q])
             else:
-                rows = nn(v_pick[k][0], recv[2, :, 0:Q])
-                rows = rows + nn(v_pick[k][1], recv[2, :, Q : 2 * Q])
-                rows = rows + nn(v_pick[k][2], recv[2, :, 2 * Q : W])
-            total = total + weights[k] * rows
-            sums[k] = sums[k] + jnp.sum(cot * rows, axis=1, keepdims=True)
-        mixed[:, Q * b : Q * b + Q] = total.astype(BF16)
+                total = nn(v_both[0], recv[3, window, 0:Q])
+                total = total + nn(v_both[1], recv[3, window, Q : 2 * Q])
+                total = total + nn(v_both[2], recv[3, window, 2 * Q : W])
+            if g == 0:
+                own[1, :, Q * b : Q * b + Q] = total
+            else:
+                part_to[1, g - 1, :, Q * b : Q * b + Q] = total.astype(BF16)
+        if g > 0:
+            parts_sent[1][g - 1].start()
+
+    for i in range(2):
+        parts_sent[0][i].wait_recv()
+        cg_sent[i].wait_recv()
+    mixed[...] = (own[0] + part_from[0, 0].astype(F32) + part_from[0, 1].astype(F32)).astype(BF16)
     leave(0, mixed, mixed_out)
-    cgrad[...] = jnp.transpose(jnp.where(iota((T, 128), 1) == 0, sums[0], sums[1]))[0:2, :]
+    cgrad[...] = (own_pair + cg_from[0] + cg_from[1])[0:2, :]
     leave(1, cgrad, cgrad_out)
 
     terms = weight_terms(c)
@@ -322,22 +433,13 @@
         out[0] = (total * grad_scale).astype(BF16)
         leave(2 + i, out, dst)
 
-    s_both = bits((lane_s == s_col[0]) | (lane_s == s_col[1]))
-    whole(3).wait_recv()
-    for b in range(3):
-        igrad[:, Q * b : Q * b + Q] = nn(s_both, recv[3, :, Q * b : Q * b + Q]).astype(BF16)
-    tail = jnp.zeros((T, Q), F32)
-    for b in range(3):
-        v_both = bits((lane_s + ROWS * b == v_col[0]) | (lane_s + ROWS * b == v_col[1]))
-        tail = tail + nn(v_both, recv[3, :, Q * b : Q * b + Q])
-    igrad[:, W:] = tail.astype(BF16)
+    for i in range(2):
+        parts_sent[1][i].wait_recv()
+    igrad[...] = (own[1] + part_from[1, 0].astype(F32) + part_from[1, 1].astype(F32)).astype(BF16)
     leave(5, igrad, igrad_out)
 
-    whole(2).wait_send()
     whole(3).wait_send()
-    for copy in over:
-        copy.wait_send()
-    for copy in hops:
+    for copy in over + hops + metas_sent + cg_sent + sum(raw_sent + parts_sent, []):
         copy.wait_send()
     for copy in left_over:
         copy.wait()
@@ -395,6 +497,13 @@
             pltpu.VMEM((CS, 3 * FF), BF16),
             pltpu.VMEM((CS, 3 * FF), BF16),
             *[pltpu.VMEM(*kind) for kind in kinds],
+            pltpu.VMEM((3, 8, T), F32),
+            pltpu.VMEM((2, 2, T, D), BF16),
+            pltpu.VMEM((2, T, D), F32),
+            pltpu.VMEM((2, 2, T, D), BF16),
+            pltpu.VMEM((2, 2, T, D), BF16),
+            pltpu.VMEM((2, 8, T), F32),
+            pltpu.VMEM((2, 8, T), F32),
             pltpu.SemaphoreType.DMA((3,)),
             pltpu.SemaphoreType.DMA((4,)),
             pltpu.SemaphoreType.DMA((4,)),
@@ -403,6 +512,14 @@
             pltpu.SemaphoreType.DMA((6,)),
             pltpu.SemaphoreType.DMA((6,)),
             pltpu.SemaphoreType.DMA((6,)),
+            pltpu.SemaphoreType.DMA((2, 2)),
+            pltpu.SemaphoreType.DMA((2, 2)),
+            pltpu.SemaphoreType.DMA((2,)),
+            pltpu.SemaphoreType.DMA((2,)),
+            pltpu.SemaphoreType.DMA((2, 2)),
+            pltpu.SemaphoreType.DMA((2, 2)),
+            pltpu.SemaphoreType.DMA((2,)),
+            pltpu.SemaphoreType.DMA((2,)),
         ],
         compiler_params=pltpu.CompilerParams(
             collective_id=0, has_side_effects=True, vmem_limit_bytes=64 << 20

time: 153 us -> 139 us (0.908)
  Pallas kernels: 152 us -> 137 us
    pallas_call x1, Pallas kernels: 150 us -> 135 us  [local(): pl.pallas_call(kernel, out_shape=outs, in_specs=[vmem, vmem, vmem, vmem,...]
where the time goes in v2:
time: 139 us; the launch traced here: 138 us
  Pallas kernels  137 us (99%)
    pallas_call x1, Pallas kernels, local(): pl.pallas_call(kernel, out_shape=outs, in_specs=[vmem, vmem, vmem, vmem,...  135 us

profile of v2, /device:TPU:32, one launch (start us, length us, event | category | flops | bytes accessed | tf_op | source)
XLA Modules:
  0.0 137.9 jit_solution(9745768713463489476)
XLA Ops:
  0.6 134.6 %expert_step.1 = (bf16[128,2048]{1,0:T(8,128)(2,1)}, bf16[128,2048]{1,0:T(8,128)(2,1)}, f32[2,128]{1,0:T(2,128)}, bf16[1,256,768]{2,1,0:T(8,128)(2,1)}, bf16[1,2...) custom-call(bf16[128,2048]{1,0:T(8,128)(2,1)} %hits.1, bf16[128,2048]{1,0:T(8,128)(2,1)} %cotangent.1, ...), custom_call_target="tpu_custom_call" | custom-call | tf_op jit(solution)/shard_map/expert_step/pallas_call | solution.py:474
  135.2 2.5 %results.1 = (bf16[128,2048]{1,0:T(8,128)(2,1)}, bf16[128,2048]{1,0:T(8,128)(2,1)}, f32[2,128]{1,0:T(2,128)}, bf16[1,256,768]{2,1,0:T(8,128)(2,1)}, bf16[1,256,7...) custom-call(bf16[128,2048]{1,0:T(8,128)(2,1)} %get-tuple-element.18.refs_0_, bf16[128,2048]{1,0:T(8,128)(2,1)} %get-tuple-element.19.refs_1_, ...), custom_call_target="tpu_custom_call" | custom-call | tf_op jit(solution)/shard_map/results/pallas_call | solution.py:529

commit v3 on v2

--- a/solution.py
+++ b/solution.py
@@ -110,22 +110,6 @@
     for other in (sibling, y_next, y_prev):
         pl.semaphore_signal(barrier, inc=1, device_id=(other, me), device_id_type=MESH)
 
-    name = iota((EXPERTS, T), 0)
-    ids = [expert_ids[k : k + 1, :] for k in range(2)]
-    named = bits((name == ids[0]) | (name == ids[1]))
-    earlier = bits(iota((T, T), 0) < iota((T, T), 1))
-    before = nn(named, earlier)
-    slots, tails = [], []
-    for k in range(2):
-        rank = jnp.sum(jnp.where(name == ids[k], before, 0.0), axis=0, keepdims=True).astype(jnp.int32)
-        block = (((ids[k] >> 2) - z) & (NZ - 1)) * NX + (((ids[k] & (NX - 1)) - x) & (NX - 1))
-        slots.append(block * RB + rank)
-        tails.append((rank >> 2) * ROWS + block * RB + CAP + (rank & 3))
-    metas[0] = jnp.concatenate(
-        [r.astype(F32) for r in slots + tails] + [combine[0:1, :], combine[1:2, :], jnp.zeros((2, T), F32)],
-        axis=0,
-    )
-
     sides = ((peer(1, 0), peer(-1, 0)), (peer(-1, 0), peer(1, 0)))
     metas_sent = [
         remote(metas.at[0], metas.at[1 + i], meta_send.at[i], meta_recv.at[i], c, sides[i][0]) for i in range(2)
@@ -143,6 +127,26 @@
     ]
     cg_sent = [remote(cg_to.at[i], cg_from.at[i], cg_send.at[i], cg_recv.at[i], c, sides[i][1]) for i in range(2)]
 
+    pl.semaphore_wait(barrier, len(near) + 3)
+    for i in range(2):
+        raw_sent[0][i].start()
+
+    name = iota((EXPERTS, T), 0)
+    ids = [expert_ids[k : k + 1, :] for k in range(2)]
+    named = bits((name == ids[0]) | (name == ids[1]))
+    earlier = bits(iota((T, T), 0) < iota((T, T), 1))
+    before = nn(named, earlier)
+    slots, tails = [], []
+    for k in range(2):
+        rank = jnp.sum(jnp.where(name == ids[k], before, 0.0), axis=0, keepdims=True).astype(jnp.int32)
+        block = (((ids[k] >> 2) - z) & (NZ - 1)) * NX + (((ids[k] & (NX - 1)) - x) & (NX - 1))
+        slots.append(block * RB + rank)
+        tails.append((rank >> 2) * ROWS + block * RB + CAP + (rank & 3))
+    metas[0] = jnp.concatenate(
+        [r.astype(F32) for r in slots + tails] + [combine[0:1, :], combine[1:2, :], jnp.zeros((2, T), F32)],
+        axis=0,
+    )
+
     def rows_of(g):
         meta = metas[g]
         return (
@@ -213,10 +217,8 @@
         copy.start()
         left_over.append(copy)
 
-    pl.semaphore_wait(barrier, len(near) + 3)
     for i in range(2):
         metas_sent[i].start()
-        raw_sent[0][i].start()
     pack_hits(0, hits)
     copies(0, False, near_blocks)
     pack_cots(0, cotangent)
@@ -283,8 +285,8 @@
 
     loads[2].wait()
     pack(lambda b: nt(hid[...], wd[Q * b : Q * b + Q, :]), send.at[2])
+    copies(2, True, range(EXPERTS))
     whole(1).wait_send()
-    copies(2, True, range(EXPERTS))
 
     whole(1).wait_recv()
     unpack(recv.at[1], cs)
@@ -303,6 +305,13 @@
             tn(xs[:, part], gu[...]),
             tn(cs[:, part], hid[...]),
         )
+
+    pack(
+        lambda b: nt(gg[...], wg[Q * b : Q * b + Q, :]) + nt(gu[...], wu[Q * b : Q * b + Q, :]),
+        send.at[3],
+    )
+
+    copies(3, True, range(EXPERTS))
 
     over = []
     for j, dy in enumerate(DYS):
@@ -312,11 +321,6 @@
         copy = remote(po.at[j], pr.at[j], po_sem.at[j], pr_sem.at[j], sibling, me)
         copy.start()
         over.append(copy)
-
-    pack(
-        lambda b: nt(gg[...], wg[Q * b : Q * b + Q, :]) + nt(gu[...], wu[Q * b : Q * b + Q, :]),
-        send.at[3],
-    )
 
     def along(i, src, dst, to):
         return remote(src, dst, y_send.at[i], y_recv.at[i], to, me)
@@ -339,8 +343,6 @@
         if j == 0:
             hops[0].start()
             hops[1].start()
-            whole(2).wait_send()
-            copies(3, True, range(EXPERTS))
         else:
             hops[1 + j].start()
 
@@ -385,8 +387,6 @@
             own_pair = pair
         else:
             cg_to[g - 1] = pair
-            parts_sent[0][g - 1].start()
-            cg_sent[g - 1].start()
 
     hops[0].wait_recv()
     st[1, top, :] = (st[1, top, :].astype(F32) + ra[...].astype(F32)).astype(BF16)
@@ -394,6 +394,12 @@
     hops[1].wait_recv()
     st[2, low, :] = (st[2, low, :].astype(F32) + rb[...].astype(F32)).astype(BF16)
     hops[5].start()
+
+    whole(2).wait_send()
+    whole(3).wait_send()
+    for i in range(2):
+        parts_sent[0][i].start()
+        cg_sent[i].start()
 
     whole(3).wait_recv()
     for g in (1, 2, 0):
@@ -438,7 +444,6 @@
     igrad[...] = (own[1] + part_from[1, 0].astype(F32) + part_from[1, 1].astype(F32)).astype(BF16)
     leave(5, igrad, igrad_out)
 
-    whole(3).wait_send()
     for copy in over + hops + metas_sent + cg_sent + sum(raw_sent + parts_sent, []):
         copy.wait_send()
     for copy in left_over:

time: 139 us -> 139 us (level)
  no operation moved by 1% of the time
where the time goes in v3:
time: 139 us; the launch traced here: 138 us
  Pallas kernels  137 us (99%)
    pallas_call x1, Pallas kernels, local(): pl.pallas_call(kernel, out_shape=outs, in_specs=[vmem, vmem, vmem, vmem,...  135 us

profile of v3, /device:TPU:32, one launch (start us, length us, event | category | flops | bytes accessed | tf_op | source)
XLA Modules:
  0.0 137.8 jit_solution(6405722030023049814)
XLA Ops:
  0.6 134.5 %expert_step.1 = (bf16[128,2048]{1,0:T(8,128)(2,1)}, bf16[128,2048]{1,0:T(8,128)(2,1)}, f32[2,128]{1,0:T(2,128)}, bf16[1,256,768]{2,1,0:T(8,128)(2,1)}, bf16[1,2...) custom-call(bf16[128,2048]{1,0:T(8,128)(2,1)} %hits.1, bf16[128,2048]{1,0:T(8,128)(2,1)} %cotangent.1, ...), custom_call_target="tpu_custom_call" | custom-call | tf_op jit(solution)/shard_map/expert_step/pallas_call | solution.py:479
  135.1 2.5 %results.1 = (bf16[128,2048]{1,0:T(8,128)(2,1)}, bf16[128,2048]{1,0:T(8,128)(2,1)}, f32[2,128]{1,0:T(2,128)}, bf16[1,256,768]{2,1,0:T(8,128)(2,1)}, bf16[1,256,7...) custom-call(bf16[128,2048]{1,0:T(8,128)(2,1)} %get-tuple-element.18.refs_0_, bf16[128,2048]{1,0:T(8,128)(2,1)} %get-tuple-element.19.refs_1_, ...), custom_call_target="tpu_custom_call" | custom-call | tf_op jit(solution)/shard_map/results/pallas_call | solution.py:534

commit v4 on v3

--- a/solution.py
+++ b/solution.py
@@ -44,9 +44,10 @@
             else:
                 table[i] = (dz - NZ + 1, dx)
     order = []
-    for dx in range(NX):
-        for dz in (4, 3, 5, 2, 6, 1, 7, 0):
-            order.append(dz * NX + dx)
+    for pair in ((2, 6), (3, 5), (4, 4), (1, 7), (0, 0)):
+        for dx in (0, 1, 2, 3) if pair[0] != pair[1] else (0, 2, 1, 3):
+            for dz in sorted(set(pair)):
+                order.append(dz * NX + dx)
     return [(i,) + table[i] for i in order if i not in SAME]
 
 

time: 139 us -> 139 us (level)
  no operation moved by 1% of the time
where the time goes in v4:
time: 139 us; the launch traced here: 138 us
  Pallas kernels  137 us (99%)
    pallas_call x1, Pallas kernels, local(): pl.pallas_call(kernel, out_shape=outs, in_specs=[vmem, vmem, vmem, vmem,...  135 us

profile of v4, /device:TPU:32, one launch (start us, length us, event | category | flops | bytes accessed | tf_op | source)
XLA Modules:
  0.0 137.8 jit_solution(13639667365518229367)
XLA Ops:
  0.6 134.5 %expert_step.1 = (bf16[128,2048]{1,0:T(8,128)(2,1)}, bf16[128,2048]{1,0:T(8,128)(2,1)}, f32[2,128]{1,0:T(2,128)}, bf16[1,256,768]{2,1,0:T(8,128)(2,1)}, bf16[1,2...) custom-call(bf16[128,2048]{1,0:T(8,128)(2,1)} %hits.1, bf16[128,2048]{1,0:T(8,128)(2,1)} %cotangent.1, ...), custom_call_target="tpu_custom_call" | custom-call | tf_op jit(solution)/shard_map/expert_step/pallas_call | solution.py:480
  135.2 2.5 %results.1 = (bf16[128,2048]{1,0:T(8,128)(2,1)}, bf16[128,2048]{1,0:T(8,128)(2,1)}, f32[2,128]{1,0:T(2,128)}, bf16[1,256,768]{2,1,0:T(8,128)(2,1)}, bf16[1,256,7...) custom-call(bf16[128,2048]{1,0:T(8,128)(2,1)} %get-tuple-element.18.refs_0_, bf16[128,2048]{1,0:T(8,128)(2,1)} %get-tuple-element.19.refs_1_, ...), custom_call_target="tpu_custom_call" | custom-call | tf_op jit(solution)/shard_map/results/pallas_call | solution.py:535
